TPU v7x, 32 devices: a whole 2x2x4 slice. The times are simulated.
32 devices in a mesh: seq: 2 (over x), ep: 16 (over z, y, core).
Axes of the slice: x: 2, y: 2, z: 4, core: 2. Of those that a mesh axis runs over, the one named last changes fastest.
Arguments:
- tokens: bfloat16 [256, 7168], P(('seq', 'ep')), may hold values from -50 to 50
- out_grad: bfloat16 [256, 7168], P(('seq', 'ep')), may hold values from -6 to 6
- routes: int32 [256, 8], P(('seq', 'ep')), may hold values from 0 to 15, all different within a row; in each aligned block of 8 rows (0 to 7, 8 to 15, ...) at most 5 rows name the same one
- gate_fixed: int32 [256, 8], P(('seq', 'ep')), may hold values from 1 to 65535
- ramp_step: int32 [16], replicated, may hold values from 1 to 8
- norm_gain: float32 [7168], replicated, may hold values from 0.1 to 1.9
- w_gate: bfloat16 [16, 7168, 1024], P('ep', None, 'seq'), may hold values from -0.0625 to 0.0625
- w_up: bfloat16 [16, 7168, 1024], P('ep', None, 'seq'), may hold values from -0.0625 to 0.0625
- w_down: bfloat16 [16, 1024, 7168], P('ep', 'seq'), may hold values from -0.1875 to 0.1875
Outputs:
- mixed: bfloat16 [256, 7168], P(('seq', 'ep'))
- tokens_grad: bfloat16 [256, 7168], P(('seq', 'ep'))
- gain_grad: float32 [7168], P(('seq', 'ep'))
- w_gate_grad: bfloat16 [16, 7168, 1024], P('ep', None, 'seq')
- w_up_grad: bfloat16 [16, 7168, 1024], P('ep', None, 'seq')
- w_down_grad: bfloat16 [16, 1024, 7168], P('ep', 'seq')
Inputs may be any that keep to these rules, and one draw needn't show every extreme that they name: `routes`: each row names 8 different experts. Within the rows of one device (aligned blocks of 8 rows) no expert is named more than 5 times, and in some such block one expert is named exactly 5 times.
All inputs are finite; a program needn't handle non-finite values.
Results may differ from a plain program's by a relative error of at most 0.023.
Values may be sent and summed in bfloat16 or wider, within the bound.
No kernel may reach another device: no remote copies, remote signals or barrier semaphores. Data moves between devices by JAX's collectives and lax.ppermute only.
A program may use at most 128 MiB of HBM per device.

v0:
```python
import jax
import jax.numpy as jnp
from jax import lax
from jax.sharding import PartitionSpec as P

RAMP = 8
gate_unit = 65536.0
norm_eps = 1e-06


def contract_rows(left, right):
    return lax.dot_general(
        left, right, (((0,), (0,)), ((), ())), preferred_element_type=jnp.float32
    )


def contract_cols(left, right):
    return lax.dot_general(
        left, right, (((1,), (1,)), ((), ())), preferred_element_type=jnp.float32
    )


def dispatch(send_normed, send_grad, seq_count, experts, capacity):
    width = send_normed.shape[1]

    def spread(buffer):
        wide = jnp.broadcast_to(
            buffer.reshape(1, experts, capacity, width), (seq_count, experts, capacity, width)
        )
        return wide.reshape(seq_count * experts, capacity, width)

    got_normed, got_grad = (
        lax.all_to_all(spread(send_normed), ("seq", "ep"), split_axis=0, concat_axis=0, tiled=True),
        lax.all_to_all(spread(send_grad), ("seq", "ep"), split_axis=0, concat_axis=0, tiled=True),
    )
    return (got_normed.reshape(-1, width), got_grad.reshape(-1, width))


def collect(out_part, back_part, seq_count, ep_count, capacity):
    width = out_part.shape[1]
    sum_out, sum_back = (
        lax.psum_scatter(
            out_part.reshape(seq_count, ep_count * capacity, width).astype(jnp.bfloat16),
            "seq",
            scatter_dimension=0,
            tiled=True,
        ).astype(jnp.float32),
        lax.psum_scatter(
            back_part.reshape(seq_count, ep_count * capacity, width).astype(jnp.bfloat16),
            "seq",
            scatter_dimension=0,
            tiled=True,
        ).astype(jnp.float32),
    )
    got_out, got_back = (
        lax.all_to_all(
            sum_out.astype(jnp.bfloat16).reshape(ep_count, capacity, width),
            "ep",
            split_axis=0,
            concat_axis=0,
            tiled=True,
        ),
        lax.all_to_all(
            sum_back.astype(jnp.bfloat16).reshape(ep_count, capacity, width),
            "ep",
            split_axis=0,
            concat_axis=0,
            tiled=True,
        ),
    )
    return (got_out.reshape(-1, width), got_back.reshape(-1, width))


def on_device(tokens, out_grad, routes, gate_fixed, ramp_step, norm_gain, w_gate, w_up, w_down):
    seq_count = lax.axis_size("seq")
    ep_count = lax.axis_size("ep")
    rows_dev, width = tokens.shape
    top_count = routes.shape[1]
    capacity = min(rows_dev, 5 * rows_dev * top_count // (4 * ep_count))
    tokens_wide = tokens.astype(jnp.float32)
    recip = lax.rsqrt(jnp.mean(tokens_wide * tokens_wide, axis=1, keepdims=True) + norm_eps)
    normed = (tokens_wide * recip * norm_gain[None, :]).astype(jnp.bfloat16)
    flat_routes = routes.reshape(-1)
    onehot = (flat_routes[:, None] == jnp.arange(ep_count, dtype=jnp.int32)[None, :]).astype(
        jnp.int32
    )
    position = jnp.sum(jnp.cumsum(onehot, axis=0) * onehot, axis=1) - 1
    slot_index = flat_routes * capacity + position
    ramp_pick = jnp.sum(onehot * ramp_step[None, :], axis=1).astype(jnp.float32)
    coef = gate_fixed.reshape(-1).astype(jnp.float32) / gate_unit * ramp_pick / RAMP
    grad_rows = (
        coef[:, None] * jnp.repeat(out_grad.astype(jnp.float32), top_count, axis=0)
    ).astype(jnp.bfloat16)
    normed_rows = jnp.repeat(normed, top_count, axis=0)
    empty = jnp.zeros((ep_count * capacity, width), jnp.bfloat16)
    send_normed = empty.at[slot_index].set(normed_rows)
    send_grad = empty.at[slot_index].set(grad_rows)
    in_normed, in_grad = dispatch(send_normed, send_grad, seq_count, ep_count, capacity)
    weight_gate = w_gate[0]
    weight_up = w_up[0]
    weight_down = w_down[0]
    pre_gate = jnp.dot(in_normed, weight_gate, preferred_element_type=jnp.float32)
    pre_up = jnp.dot(in_normed, weight_up, preferred_element_type=jnp.float32)
    sigma = jax.nn.sigmoid(pre_gate)
    active = pre_gate * sigma
    hidden = (active * pre_up).astype(jnp.bfloat16)
    out_part = jnp.dot(hidden, weight_down, preferred_element_type=jnp.float32)
    hidden_grad = contract_cols(in_grad, weight_down)
    gate_pre_grad = (hidden_grad * pre_up * sigma * (1.0 + pre_gate * (1.0 - sigma))).astype(
        jnp.bfloat16
    )
    up_pre_grad = (hidden_grad * active).astype(jnp.bfloat16)
    w_down_grad = contract_rows(hidden, in_grad).astype(jnp.bfloat16)[None]
    w_gate_grad = contract_rows(in_normed, gate_pre_grad).astype(jnp.bfloat16)[None]
    w_up_grad = contract_rows(in_normed, up_pre_grad).astype(jnp.bfloat16)[None]
    back_part = contract_cols(gate_pre_grad, weight_gate) + contract_cols(up_pre_grad, weight_up)
    slot_out, slot_back = collect(out_part, back_part, seq_count, ep_count, capacity)
    picked_out = slot_out[slot_index].astype(jnp.float32).reshape(rows_dev, top_count, width)
    picked_back = slot_back[slot_index].astype(jnp.float32).reshape(rows_dev, top_count, width)
    mixed = jnp.sum(coef.reshape(rows_dev, top_count, 1) * picked_out, axis=1).astype(jnp.bfloat16)
    normed_grad = jnp.sum(picked_back, axis=1)
    gain_term = jnp.sum(normed_grad * tokens_wide * recip, axis=0)
    gain_grad = lax.psum_scatter(gain_term, ("seq", "ep"), scatter_dimension=0, tiled=True)
    scaled = norm_gain[None, :] * normed_grad
    inner = jnp.sum(scaled * tokens_wide, axis=1, keepdims=True)
    tokens_grad = (recip * scaled - tokens_wide * recip * recip * recip * inner / width).astype(
        jnp.bfloat16
    )
    return (mixed, tokens_grad, gain_grad, w_gate_grad, w_up_grad, w_down_grad)


def solution(mesh):
    return jax.shard_map(
        on_device,
        mesh=mesh,
        in_specs=(
            P(("seq", "ep"), None),
            P(("seq", "ep"), None),
            P(("seq", "ep"), None),
            P(("seq", "ep"), None),
            P(),
            P(),
            P("ep", None, "seq"),
            P("ep", None, "seq"),
            P("ep", "seq", None),
        ),
        out_specs=(
            P(("seq", "ep"), None),
            P(("seq", "ep"), None),
            P(("seq", "ep")),
            P("ep", None, "seq"),
            P("ep", None, "seq"),
            P("ep", "seq", None),
        ),
        check_vma=False,
    )
```

profile of v0, /device:TPU:0, one launch (start us, length us, event | category | flops | bytes accessed | tf_op | source)
XLA Modules:
  0.0 395.7 jit_solution(4662358553127045000)
XLA Ops:
  7.2 0.8 eq.15
  7.9 0.7 broadcast_multiply_fusion
  8.6 1.1 fusion.34
  9.7 0.1 mul.148
  9.8 0.1 fusion.38
  9.9 0.1 reduce_window_sum.11
  10.0 0.8 select_reduce_fusion.1
  10.8 1.0 fusion.28
  11.8 2.2 scatter_custom_fusion
  14.0 0.6 broadcast_in_dim.22
  14.6 2.3 broadcast_in_dim.46
  16.8 0.0 copy-start.3
  16.8 0.0 copy-start.2
  16.8 7.4 %all-to-all-start = ((bf16[32,5,7168]{2,1,0:T(8,128)(2,1)}), bf16[32,5,7168]{2,1,0:T(8,128)(2,1)}, u32[]{:S(2)}, u32[]{:S(2)}) async-start(bf16[32,5,7168]{2,1,0:T(8,128)(2,1)} %bitcast.62), calls=%async_computation | async-start | bytes 7340032 | tf_op jit(solution)/shard_map/all_to_all | solution.py:33
  24.3 0.1 convert_element_type.90
  24.3 0.0 copy-done.3
  24.4 0.1 div.36
  24.4 0.0 copy-done.2
  24.5 2.2 scatter_custom_fusion.1
  26.7 0.6 broadcast_in_dim.48
  27.3 80.6 %all-to-all-done = bf16[32,5,7168]{2,1,0:T(8,128)(2,1)} async-done(((bf16[32,5,7168]{2,1,0:T(8,128)(2,1)}), bf16[32,5,7168]{2,1,0:T(8,128)(2,1)}, u32[]{:S(2)}, u32[]{:S(2)}) %all-to-all-start) | async-done | bytes 2293792 | tf_op jit(solution)/shard_map/all_to_all | solution.py:33
  107.8 2.2 broadcast_in_dim.49
  110.1 3.5 all-to-all-start.2
  113.6 0.0 reduce-scatter.3.cloned.1.call-start
  113.7 3.3 reshape.132
  117.0 4.4 %fusion.8 = f32[160,512]{1,0:T(8,128)S(1)} fusion(bf16[160,7168]{1,0:T(8,128)(2,1)S(1)} %reshape.132, bf16[1,7168,512]{2,1,0:T(8,128)(2,1)} %param.16), kind=kOutput, calls=%fused_computation.17 | convolution fusion | flops 1174405120 | bytes 9961472 | tf_op jit(solution)/shard_map/dot_general | solution.py:103
  121.4 4.4 %fusion.12 = f32[160,512]{1,0:T(8,128)S(1)} fusion(bf16[160,7168]{1,0:T(8,128)(2,1)S(1)} %reshape.132, bf16[1,7168,512]{2,1,0:T(8,128)(2,1)} %param.15), kind=kOutput, calls=%fused_computation.21 | convolution fusion | flops 1174405120 | bytes 9961472 | tf_op jit(solution)/shard_map/dot_general | solution.py:102
  125.8 71.4 %all-to-all-done.2 = bf16[32,5,7168]{2,1,0:T(8,128)(2,1)} async-done(((bf16[32,5,7168]{2,1,0:T(8,128)(2,1)}), bf16[32,5,7168]{2,1,0:T(8,128)(2,1)}, u32[]{:S(2)}, u32[]{:S(2)}) %all-to-all-start.2) | async-done | bytes 2293792 | tf_op jit(solution)/shard_map/all_to_all | solution.py:34
  197.3 4.6 %reshape.137 = bf16[160,7168]{1,0:T(8,128)(2,1)} reshape(bf16[32,5,7168]{2,1,0:T(8,128)(2,1)} %all-to-all-done.2) | data formatting | bytes 4587520 | tf_op jit(solution)/shard_map/reshape | solution.py:36
  201.8 6.4 %multiply_convert_fusion = (bf16[160,512]{1,0:T(8,128)(2,1)S(1)}, bf16[160,512]{1,0:T(8,128)(2,1)S(1)}, bf16[160,512]{1,0:T(8,128)(2,1)S(1)}) fusion(f32[160,512]{1,0:T(8,128)S(1)} %fusion.12, f32[160,512]{1,0:T(8,128)S(1)} %fusion.8, bf16[160,7168]{1,0:T(8,128)(2,1)} %reshape.137, bf16[1,512,7168]{2,1,0:T(8,128)(2,1)} %param.17), kind=kOutput, calls=%fused_computation.40 | convolution fusion | flops 1175633920 | bytes 10780672 | tf_op jit(solution)/shard_map/dot_general | solution.py:18
  208.3 5.8 %convolution_convert_fusion.3 = bf16[2,80,7168]{2,1,0:T(8,128)(2,1)} fusion(bf16[2,80,512]{2,1,0:T(8,128)(2,1)S(1)} %bitcast.65, bf16[1,512,7168]{2,1,0:T(8,128)(2,1)} %param.17), kind=kOutput, calls=%fused_computation.12 | convolution fusion | flops 1175552000 | bytes 9797632 | tf_op jit(solution)/shard_map/dot_general | solution.py:107
  214.1 0.0 reduce-scatter.3.cloned.1.call-update
  214.1 0.2 reduce-scatter.5.cloned.1.call-start
  214.4 5.8 %fusion.10 = f32[160,7168]{1,0:T(8,128)S(1)} fusion(bf16[160,512]{1,0:T(8,128)(2,1)S(1)} %get-tuple-element.11, bf16[1,7168,512]{2,1,0:T(8,128)(2,1)} %param.15), kind=kOutput, calls=%fused_computation.19 | convolution fusion | flops 1174405120 | bytes 12091392 | tf_op jit(solution)/shard_map/dot_general | solution.py:18
  220.2 7.1 %fusion.3 = bf16[160,7168]{1,0:T(8,128)(2,1)} fusion(f32[160,7168]{1,0:T(8,128)S(1)} %fusion.10, bf16[160,512]{1,0:T(8,128)(2,1)S(1)} %get-tuple-element.10, bf16[1,7168,512]{2,1,0:T(8,128)(2,1)} %param.16), kind=kOutput, calls=%fused_computation.11 | convolution fusion | flops 1176698880 | bytes 14385152 | tf_op jit(solution)/shard_map/dot_general | solution.py:18
  227.2 0.0 reduce-scatter.5.cloned.1.call-update
  227.3 18.1 %reduce-scatter.3.cloned.1.call-done = bf16[1,80,7168]{2,1,0:T(8,128)(2,1)} async-done(((bf16[2,80,7168]{2,1,0:T(8,128)(2,1)}), bf16[1,80,7168]{2,1,0:T(8,128)(2,1)}) %reduce-scatter.3.cloned.1.call-update) | async-done | bytes 1146896 | tf_op jit(solution)/shard_map/reduce_scatter | solution.py:42
  245.4 2.5 reshape.133
  247.9 5.7 %all-to-all-start.1 = ((bf16[16,5,7168]{2,1,0:T(8,128)(2,1)}), bf16[16,5,7168]{2,1,0:T(8,128)(2,1)}, u32[]{:S(2)}, u32[]{:S(2)}) async-start(bf16[16,5,7168]{2,1,0:T(8,128)(2,1)} %reshape.133), calls=%async_computation.2 | async-start | bytes 3670016 | tf_op jit(solution)/shard_map/all_to_all | solution.py:56
  253.6 28.7 %reduce-scatter.5.cloned.1.call-done = bf16[1,80,7168]{2,1,0:T(8,128)(2,1)} async-done(((bf16[2,80,7168]{2,1,0:T(8,128)(2,1)}), bf16[1,80,7168]{2,1,0:T(8,128)(2,1)}) %reduce-scatter.5.cloned.1.call-update) | async-done | bytes 1146896 | tf_op jit(solution)/shard_map/reduce_scatter | solution.py:48
  282.3 2.5 reshape.138
  284.8 5.2 %all-to-all-done.1 = bf16[16,5,7168]{2,1,0:T(8,128)(2,1)} async-done(((bf16[16,5,7168]{2,1,0:T(8,128)(2,1)}), bf16[16,5,7168]{2,1,0:T(8,128)(2,1)}, u32[]{:S(2)}, u32[]{:S(2)}) %all-to-all-start.1) | async-done | bytes 1146912 | tf_op jit(solution)/shard_map/all_to_all | solution.py:56
  290.1 10.2 %all-to-all-start.3 = ((bf16[16,5,7168]{2,1,0:T(8,128)(2,1)}), bf16[16,5,7168]{2,1,0:T(8,128)(2,1)}, u32[]{:S(2)}, u32[]{:S(2)}) async-start(bf16[16,5,7168]{2,1,0:T(8,128)(2,1)} %reshape.138), calls=%async_computation.5 | async-start | bytes 3670016 | tf_op jit(solution)/shard_map/all_to_all | solution.py:63
  300.3 6.8 %fusion.2 = bf16[1,512,7168]{2,1,0:T(8,128)(2,1)} fusion(bf16[160,512]{1,0:T(8,128)(2,1)S(1)} %get-tuple-element.12, bf16[160,7168]{1,0:T(8,128)(2,1)} %reshape.137), kind=kOutput, calls=%fused_computation.9 | convolution fusion | flops 1178075136 | bytes 9797632 | tf_op jit(solution)/shard_map/dot_general | solution.py:12
  307.1 5.2 %fusion.1 = bf16[1,7168,512]{2,1,0:T(8,128)(2,1)} fusion(bf16[160,7168]{1,0:T(8,128)(2,1)S(1)} %reshape.132, bf16[160,512]{1,0:T(8,128)(2,1)S(1)} %get-tuple-element.10), kind=kOutput, calls=%fused_computation.8 | convolution fusion | flops 1178075136 | bytes 9797632 | tf_op jit(solution)/shard_map/dot_general | solution.py:12
  312.3 5.2 %fusion = bf16[1,7168,512]{2,1,0:T(8,128)(2,1)} fusion(bf16[160,7168]{1,0:T(8,128)(2,1)S(1)} %reshape.132, bf16[160,512]{1,0:T(8,128)(2,1)S(1)} %get-tuple-element.11), kind=kOutput, calls=%fused_computation.7 | convolution fusion | flops 1178075136 | bytes 9797632 | tf_op jit(solution)/shard_map/dot_general | solution.py:12
  317.4 1.7 reshape.134
  319.2 1.1 gather_fusion
  320.3 16.4 %all-to-all-done.3 = bf16[16,5,7168]{2,1,0:T(8,128)(2,1)} async-done(((bf16[16,5,7168]{2,1,0:T(8,128)(2,1)}), bf16[16,5,7168]{2,1,0:T(8,128)(2,1)}, u32[]{:S(2)}, u32[]{:S(2)}) %all-to-all-start.3) | async-done | bytes 1146912 | tf_op jit(solution)/shard_map/all_to_all | solution.py:63
  336.7 1.7 reshape.139
  338.5 0.0 copy-start
  338.5 0.0 copy-start.1
  338.5 1.1 gather_fusion.1
  339.6 0.6 convert_reduce_fusion
  340.2 0.0 copy-done
  340.3 0.0 copy-done.1
  340.3 0.2 fusion.37
  340.5 0.8 fusion.33
  341.3 45.5 %all-reduce = f32[7168]{0:T(1024)S(1)} all-reduce(f32[7168]{0:T(1024)S(1)} %get-tuple-element.6), channel_id=4, replica_groups=mesh['seq'=2,'ep'=16] {'seq','ep'}, use_global_device_ids=true, to_apply=%region_12.13.clone | all-reduce | flops 7168 | bytes 57344
  386.8 1.4 fusion.14
  388.2 0.6 dynamic-slice
  (7 shorter events, 0.1 us)
Async XLA Ops:
  16.8 7.5 %copy-start.3 = (s32[8,8]{1,0:T(8,128)S(1)}, s32[8,8]{1,0:T(8,128)}, u32[]{:S(2)}) copy-start(s32[8,8]{1,0:T(8,128)} %param.12) | copy-start | bytes 772
  16.8 7.6 %copy-start.2 = (bf16[8,7168]{1,0:T(8,128)(2,1)S(1)}, bf16[8,7168]{1,0:T(8,128)(2,1)}, u32[]{:S(2)}) copy-start(bf16[8,7168]{1,0:T(8,128)(2,1)} %param.10) | copy-start | bytes 344068
  16.8 91.0 %all-to-all-start = ((bf16[32,5,7168]{2,1,0:T(8,128)(2,1)}), bf16[32,5,7168]{2,1,0:T(8,128)(2,1)}, u32[]{:S(2)}, u32[]{:S(2)}) async-start(bf16[32,5,7168]{2,1,0:T(8,128)(2,1)} %bitcast.62), calls=%async_computation | async-start | bytes 7340032 | tf_op jit(solution)/shard_map/all_to_all | solution.py:33
  110.1 87.2 %all-to-all-start.2 = ((bf16[32,5,7168]{2,1,0:T(8,128)(2,1)}), bf16[32,5,7168]{2,1,0:T(8,128)(2,1)}, u32[]{:S(2)}, u32[]{:S(2)}) async-start(bf16[32,5,7168]{2,1,0:T(8,128)(2,1)} %bitcast.63), calls=%async_computation.3 | async-start | bytes 7340032 | tf_op jit(solution)/shard_map/all_to_all | solution.py:34
  113.6 131.7 %reduce-scatter.3.cloned.1.call-start = ((), (), s32[]{:S(2)}) async-start(), calls=%async_computation.6 | async-start | bytes 3440640 | tf_op jit(solution)/shard_map/reduce_scatter | solution.py:42
  214.1 68.2 %reduce-scatter.5.cloned.1.call-start = ((), (), s32[]{:S(2)}) async-start(), calls=%async_computation.7 | async-start | bytes 3440640 | tf_op jit(solution)/shard_map/reduce_scatter | solution.py:48
  247.9 42.1 %all-to-all-start.1 = ((bf16[16,5,7168]{2,1,0:T(8,128)(2,1)}), bf16[16,5,7168]{2,1,0:T(8,128)(2,1)}, u32[]{:S(2)}, u32[]{:S(2)}) async-start(bf16[16,5,7168]{2,1,0:T(8,128)(2,1)} %reshape.133), calls=%async_computation.2 | async-start | bytes 3670016 | tf_op jit(solution)/shard_map/all_to_all | solution.py:56
  290.1 46.7 %all-to-all-start.3 = ((bf16[16,5,7168]{2,1,0:T(8,128)(2,1)}), bf16[16,5,7168]{2,1,0:T(8,128)(2,1)}, u32[]{:S(2)}, u32[]{:S(2)}) async-start(bf16[16,5,7168]{2,1,0:T(8,128)(2,1)} %reshape.138), calls=%async_computation.5 | async-start | bytes 3670016 | tf_op jit(solution)/shard_map/all_to_all | solution.py:63
  338.5 1.8 copy-start
  338.5 1.8 copy-start.1
Sparse Core Ops, SparseCore 0:
  214.3 31.0 reduce-scatter.2
  248.2 34.0 reduce-scatter.4
where the time goes:
time: 397 us; the launch traced here: 396 us
  waiting for transfers between devices  220 us (55%)
  matrix products  51.1 us (13%)
  blocking collectives  45.5 us (11%)
  local copies, waits for them, and re-layouts  28.1 us (7%)
  starting transfers between devices  27.1 us (7%)
  between operations  14.3 us (4%)
  other arithmetic  9.08 us (2%)
    all_to_all x1, waiting for transfers between devices, dispatch(): lax.all_to_all(spread(send_normed), ('seq', 'ep'), split_axis=0, concat_a...  80.6 us
    all_to_all x1, waiting for transfers between devices, dispatch(): lax.all_to_all(spread(send_grad), ('seq', 'ep'), split_axis=0, concat_axi...  71.4 us
    unnamed x1, blocking collectives  45.5 us
    reduce_scatter x1, waiting for transfers between devices, collect(): lax.psum_scatter(back_part.reshape(seq_count, ep_count * capacity, width)...  28.7 us
    dot_general x3, matrix products, contract_cols(): lax.dot_general(left, right, (((1,), (1,)), ((), ())), preferred_element_...  19.3 us
    reduce_scatter x1, waiting for transfers between devices, collect(): lax.psum_scatter(out_part.reshape(seq_count, ep_count * capacity, width)....  18.1 us
    dot_general x3, matrix products, contract_rows(): lax.dot_general(left, right, (((0,), (0,)), ((), ())), preferred_element_...  17.1 us
    all_to_all x1, waiting for transfers between devices, collect(): lax.all_to_all(sum_back.astype(jnp.bfloat16).reshape(ep_count, capacity,...  16.4 us
  transfers between devices with their start and end apart: 6, of which 6 were waited for; matrix products, arithmetic and copies ran while one was open for 13% of the time, Pallas kernels for 0%

commit v1 on v0

--- a/solution.py
+++ b/solution.py
@@ -6,6 +6,30 @@
 RAMP = 8
 gate_unit = 65536.0
 norm_eps = 1e-06
+
+
+def split_up(x, dim, count):
+    lengths = x.shape
+    tiles = x.reshape(*lengths[:dim], count, lengths[dim] // count, *lengths[dim + 1 :])
+    return jnp.moveaxis(tiles, dim, 0)
+
+
+def joined_along(blocks, dim):
+    shape = list(blocks.shape[1:])
+    shape[dim] *= blocks.shape[0]
+    return jnp.moveaxis(blocks, 0, dim).reshape(shape)
+
+
+def sent_to_each(x, axis, split_dim, concat_dim):
+    count, place = (lax.axis_size(axis), lax.axis_index(axis))
+    parts = split_up(x, split_dim, count)
+    whole = parts
+    for step in range(1, count):
+        target, source = ((place + step) % count, (place - step) % count)
+        sent = lax.dynamic_index_in_dim(parts, target, 0)
+        received = lax.ppermute(sent, axis, [(i, (i + step) % count) for i in range(count)])
+        whole = lax.dynamic_update_slice_in_dim(whole, received, source, axis=0)
+    return joined_along(whole, concat_dim)
 
 
 def contract_rows(left, right):
@@ -60,13 +84,7 @@
             concat_axis=0,
             tiled=True,
         ),
-        lax.all_to_all(
-            sum_back.astype(jnp.bfloat16).reshape(ep_count, capacity, width),
-            "ep",
-            split_axis=0,
-            concat_axis=0,
-            tiled=True,
-        ),
+        sent_to_each(sum_back.astype(jnp.bfloat16).reshape(ep_count, capacity, width), "ep", 0, 0),
     )
     return (got_out.reshape(-1, width), got_back.reshape(-1, width))
 

time: 397 us -> 458 us (1.15)
  waiting for transfers between devices: 220 us -> 259 us
  starting transfers between devices: 27.1 us -> 42.2 us
  local copies, waits for them, and re-layouts: 28.1 us -> 40.9 us
    ppermute x0 -> x15, waiting for transfers between devices: none -> 70.6 us  [sent_to_each(): lax.ppermute(sent, axis, [(i, (i + step) % count) for i in range(count)])]
    ppermute x0 -> x15, starting transfers between devices: none -> 25.1 us  [sent_to_each(): lax.ppermute(sent, axis, [(i, (i + step) % count) for i in range(count)])]
    all_to_all x1 -> x0, waiting for transfers between devices: 16.4 us -> none  [collect(): lax.all_to_all(sum_back.astype(jnp.bfloat16).reshape(ep_count, capacity,...]
    reduce_scatter x1, waiting for transfers between devices: 28.7 us -> 17.8 us  [collect(): lax.psum_scatter(back_part.reshape(seq_count, ep_count * capacity, width)...]
    all_to_all x1 -> x0, starting transfers between devices: 10.2 us -> none  [collect(): lax.all_to_all(sum_back.astype(jnp.bfloat16).reshape(ep_count, capacity,...]
    dynamic_update_slice x0 -> x14, local copies, waits for them, and re-layouts: none -> 9.17 us  [sent_to_each(): whole = lax.dynamic_update_slice_in_dim(whole, received, source, axis=0)]
    all_to_all x1, waiting for transfers between devices: 5.21 us -> 0.01 us  [collect(): lax.all_to_all(sum_out.astype(jnp.bfloat16).reshape(ep_count, capacity, w...]
  transfers between devices with their start and end apart: 6 -> 20, of which waited for: 6 -> 14; matrix products, arithmetic and copies ran while one was open for 13% -> 13% of each run, Pallas kernels for 0% -> 0%
where the time goes in v1:
time: 458 us; the launch traced here: 457 us
  waiting for transfers between devices  259 us (57%)
  matrix products  48.4 us (11%)
  blocking collectives  43 us (9%)
  starting transfers between devices  42.2 us (9%)
  local copies, waits for them, and re-layouts  40.9 us (9%)
  between operations  15 us (3%)
  other arithmetic  9.08 us (2%)
    all_to_all x1, waiting for transfers between devices, dispatch(): lax.all_to_all(spread(send_normed), ('seq', 'ep'), split_axis=0, concat_a...  80.6 us
    all_to_all x1, waiting for transfers between devices, dispatch(): lax.all_to_all(spread(send_grad), ('seq', 'ep'), split_axis=0, concat_axi...  71.2 us
    ppermute x15, waiting for transfers between devices, sent_to_each(): lax.ppermute(sent, axis, [(i, (i + step) % count) for i in range(count)])  70.6 us
    unnamed x1, blocking collectives  43 us
    ppermute x15, starting transfers between devices, sent_to_each(): lax.ppermute(sent, axis, [(i, (i + step) % count) for i in range(count)])  25.1 us
    reduce_scatter x1, waiting for transfers between devices, collect(): lax.psum_scatter(out_part.reshape(seq_count, ep_count * capacity, width)....  18.3 us
    reduce_scatter x1, waiting for transfers between devices, collect(): lax.psum_scatter(back_part.reshape(seq_count, ep_count * capacity, width)...  17.8 us
    dot_general x3, matrix products, contract_rows(): lax.dot_general(left, right, (((0,), (0,)), ((), ())), preferred_element_...  17.2 us
  transfers between devices with their start and end apart: 20, of which 14 were waited for; matrix products, arithmetic and copies ran while one was open for 13% of the time, Pallas kernels for 0%

profile of v1, /device:TPU:0, one launch (start us, length us, event | category | flops | bytes accessed | tf_op | source)
XLA Modules:
  0.0 457.1 jit_solution(10134265108688122662)
XLA Ops:
  7.2 0.8 eq.46
  7.9 0.7 broadcast_multiply_fusion
  8.6 1.1 fusion.34
  10.0 0.8 select_reduce_fusion.1
  10.8 1.0 fusion.28
  11.8 2.2 scatter_custom_fusion
  14.6 2.4 broadcast_in_dim.46
  16.9 7.4 %all-to-all-start = ((bf16[32,5,7168]{2,1,0:T(8,128)(2,1)}), bf16[32,5,7168]{2,1,0:T(8,128)(2,1)}, u32[]{:S(2)}, u32[]{:S(2)}) async-start(bf16[32,5,7168]{2,1,0:T(8,128)(2,1)} %bitcast.66), calls=%async_computation | async-start | bytes 7340032 | tf_op jit(solution)/shard_map/all_to_all | solution.py:57
  24.6 2.2 scatter_custom_fusion.1
  27.4 80.6 %all-to-all-done = bf16[32,5,7168]{2,1,0:T(8,128)(2,1)} async-done(((bf16[32,5,7168]{2,1,0:T(8,128)(2,1)}), bf16[32,5,7168]{2,1,0:T(8,128)(2,1)}, u32[]{:S(2)}, u32[]{:S(2)}) %all-to-all-start) | async-done | bytes 2293792 | tf_op jit(solution)/shard_map/all_to_all | solution.py:57
  108.0 2.4 broadcast_in_dim.49
  110.4 3.5 all-to-all-start.2
  114.1 3.3 reshape.126
  117.4 4.4 fusion.8
  121.8 4.4 fusion.12
  126.3 71.2 %all-to-all-done.2 = bf16[32,5,7168]{2,1,0:T(8,128)(2,1)} async-done(((bf16[32,5,7168]{2,1,0:T(8,128)(2,1)}), bf16[32,5,7168]{2,1,0:T(8,128)(2,1)}, u32[]{:S(2)}, u32[]{:S(2)}) %all-to-all-start.2) | async-done | bytes 2293792 | tf_op jit(solution)/shard_map/all_to_all | solution.py:58
  197.5 4.6 %reshape.131 = bf16[160,7168]{1,0:T(8,128)(2,1)} reshape(bf16[32,5,7168]{2,1,0:T(8,128)(2,1)} %all-to-all-done.2) | data formatting | bytes 4587520 | tf_op jit(solution)/shard_map/reshape | solution.py:60
  202.1 6.6 %multiply_convert_fusion = (bf16[160,512]{1,0:T(8,128)(2,1)S(1)}, bf16[160,512]{1,0:T(8,128)(2,1)S(1)}, bf16[160,512]{1,0:T(8,128)(2,1)S(1)}) fusion(f32[160,512]{1,0:T(8,128)S(1)} %fusion.12, f32[160,512]{1,0:T(8,128)S(1)} %fusion.8, bf16[160,7168]{1,0:T(8,128)(2,1)} %reshape.131, bf16[1,512,7168]{2,1,0:T(8,128)(2,1)} %param.17), kind=kOutput, calls=%fused_computation.40 | convolution fusion | flops 1175633920 | bytes 10780672 | tf_op jit(solution)/shard_map/dot_general | solution.py:42
  208.7 5.8 %fusion.10 = f32[160,7168]{1,0:T(8,128)S(1)} fusion(bf16[160,512]{1,0:T(8,128)(2,1)S(1)} %get-tuple-element.26, bf16[1,7168,512]{2,1,0:T(8,128)(2,1)} %param.15), kind=kOutput, calls=%fused_computation.19 | convolution fusion | flops 1174405120 | bytes 12091392 | tf_op jit(solution)/shard_map/dot_general | solution.py:42
  214.5 4.0 fusion.3
  218.6 5.9 %convolution_convert_fusion.3 = bf16[2,80,7168]{2,1,0:T(8,128)(2,1)} fusion(bf16[2,80,512]{2,1,0:T(8,128)(2,1)S(1)} %bitcast.69, bf16[1,512,7168]{2,1,0:T(8,128)(2,1)} %param.17), kind=kOutput, calls=%fused_computation.12 | convolution fusion | flops 1175552000 | bytes 9797632 | tf_op jit(solution)/shard_map/dot_general | solution.py:125
  225.1 6.8 %fusion.2 = bf16[1,512,7168]{2,1,0:T(8,128)(2,1)} fusion(bf16[160,512]{1,0:T(8,128)(2,1)S(1)} %get-tuple-element.27, bf16[160,7168]{1,0:T(8,128)(2,1)} %reshape.131), kind=kOutput, calls=%fused_computation.9 | convolution fusion | flops 1178075136 | bytes 9797632 | tf_op jit(solution)/shard_map/dot_general | solution.py:36
  231.9 17.8 %reduce-scatter.5.cloned.1.call-done = bf16[1,80,7168]{2,1,0:T(8,128)(2,1)} async-done(((bf16[2,80,7168]{2,1,0:T(8,128)(2,1)}), bf16[1,80,7168]{2,1,0:T(8,128)(2,1)}) %reduce-scatter.5.cloned.1.call-update) | async-done | bytes 1146896 | tf_op jit(solution)/shard_map/reduce_scatter | solution.py:72
  249.8 2.6 reshape_reshape.6
  252.4 0.9 constant_dynamic-slice_fusion.14
  253.3 5.3 %fusion.1 = bf16[1,7168,512]{2,1,0:T(8,128)(2,1)} fusion(bf16[160,7168]{1,0:T(8,128)(2,1)S(1)} %reshape.126, bf16[160,512]{1,0:T(8,128)(2,1)S(1)} %get-tuple-element.25), kind=kOutput, calls=%fused_computation.8 | convolution fusion | flops 1178075136 | bytes 9797632 | tf_op jit(solution)/shard_map/dot_general | solution.py:36
  258.6 1.6 collective-permute-done
  260.2 2.4 constant_dynamic-slice_fusion
  262.7 5.2 %fusion = bf16[1,7168,512]{2,1,0:T(8,128)(2,1)} fusion(bf16[160,7168]{1,0:T(8,128)(2,1)S(1)} %reshape.126, bf16[160,512]{1,0:T(8,128)(2,1)S(1)} %get-tuple-element.26), kind=kOutput, calls=%fused_computation.7 | convolution fusion | flops 1178075136 | bytes 9797632 | tf_op jit(solution)/shard_map/dot_general | solution.py:36
  267.8 18.3 %reduce-scatter.3.cloned.1.call-done = bf16[1,80,7168]{2,1,0:T(8,128)(2,1)} async-done(((bf16[2,80,7168]{2,1,0:T(8,128)(2,1)}), bf16[1,80,7168]{2,1,0:T(8,128)(2,1)}) %reduce-scatter.3.cloned.1.call-update) | async-done | bytes 1146896 | tf_op jit(solution)/shard_map/reduce_scatter | solution.py:66
  286.1 2.6 reshape.127
  288.8 5.8 %all-to-all-start.1 = ((bf16[16,5,7168]{2,1,0:T(8,128)(2,1)}), bf16[16,5,7168]{2,1,0:T(8,128)(2,1)}, u32[]{:S(2)}, u32[]{:S(2)}) async-start(bf16[16,5,7168]{2,1,0:T(8,128)(2,1)} %reshape.127), calls=%async_computation.2 | async-start | bytes 3670016 | tf_op jit(solution)/shard_map/all_to_all | solution.py:80
  294.6 4.3 collective-permute-start.14
  300.1 1.4 collective-permute-start.2
  302.1 36.2 %collective-permute-done.2 = bf16[1,1,5,7168]{3,2,0,1:T(8,128)(2,1)S(1)} collective-permute-done((bf16[1,1,5,7168]{3,2,0,1:T(8,128)(2,1)S(1)}, bf16[1,1,5,7168]{3,2,0,1:T(8,128)(2,1)S(1)}, u32[]{:S(2)}, u32[]{:S(2)}) %collective-permute-start.2) | collective-permute-done | bytes 71712 | tf_op jit(solution)/shard_map/ppermute | solution.py:30
  339.0 6.0 %collective-permute-done.3 = bf16[1,1,5,7168]{3,2,0,1:T(8,128)(2,1)S(1)} collective-permute-done((bf16[1,1,5,7168]{3,2,0,1:T(8,128)(2,1)S(1)}, bf16[1,1,5,7168]{3,2,0,1:T(8,128)(2,1)S(1)}, u32[]{:S(2)}, u32[]{:S(2)}) %collective-permute-start.3) | collective-permute-done | bytes 71712 | tf_op jit(solution)/shard_map/ppermute | solution.py:30
  345.0 5.1 %collective-permute-start.4 = (bf16[1,1,5,7168]{3,2,0,1:T(8,128)(2,1)S(1)}, bf16[1,1,5,7168]{3,2,0,1:T(8,128)(2,1)S(1)}, u32[]{:S(2)}, u32[]{:S(2)}) collective-permute-start(bf16[1,1,5,7168]{3,2,0,1:T(8,128)(2,1)S(1)} %copy-done.6), channel_id=1, source_target_pairs={{0,5},{1,6},{2,7},{3,8},{4,9},{5,10},{6,11},{7,12},{8,13},{9,14},{... | collective-permute-start | bytes 215048 | tf_op jit(solution)/shard_map/ppermute | solution.py:30
  350.1 0.7 constant_dynamic-update-slice_fusion.10
  350.8 1.7 collective-permute-done.4
  352.5 1.1 collective-permute-start.5
  354.2 6.5 %collective-permute-done.5 = bf16[1,1,5,7168]{3,2,0,1:T(8,128)(2,1)S(1)} collective-permute-done((bf16[1,1,5,7168]{3,2,0,1:T(8,128)(2,1)S(1)}, bf16[1,1,5,7168]{3,2,0,1:T(8,128)(2,1)S(1)}, u32[]{:S(2)}, u32[]{:S(2)}) %collective-permute-start.5) | collective-permute-done | bytes 71712 | tf_op jit(solution)/shard_map/ppermute | solution.py:30
  360.7 0.7 constant_dynamic-update-slice_fusion.8
  361.3 4.5 collective-permute-done.6
  365.8 5.4 %collective-permute-start.7 = (bf16[1,1,5,7168]{3,2,0,1:T(8,128)(2,1)S(1)}, bf16[1,1,5,7168]{3,2,0,1:T(8,128)(2,1)S(1)}, u32[]{:S(2)}, u32[]{:S(2)}) collective-permute-start(bf16[1,1,5,7168]{3,2,0,1:T(8,128)(2,1)S(1)} %copy-done.3), channel_id=1, source_target_pairs={{0,8},{1,9},{2,10},{3,11},{4,12},{5,13},{6,14},{7,15},{8,0},{9,1},... | collective-permute-start | bytes 215048 | tf_op jit(solution)/shard_map/ppermute | solution.py:30
  371.2 0.7 constant_dynamic-update-slice_fusion.7
  371.9 5.3 %collective-permute-done.7 = bf16[1,1,5,7168]{3,2,0,1:T(8,128)(2,1)S(1)} collective-permute-done((bf16[1,1,5,7168]{3,2,0,1:T(8,128)(2,1)S(1)}, bf16[1,1,5,7168]{3,2,0,1:T(8,128)(2,1)S(1)}, u32[]{:S(2)}, u32[]{:S(2)}) %collective-permute-start.7) | collective-permute-done | bytes 71712 | tf_op jit(solution)/shard_map/ppermute | solution.py:30
  377.1 0.7 constant_dynamic-update-slice_fusion.6
  377.8 4.5 collective-permute-done.8
  382.3 2.8 collective-permute-start.9
  385.1 0.7 constant_dynamic-update-slice_fusion.5
  385.7 2.6 collective-permute-done.9
  388.4 3.7 collective-permute-start.10
  392.1 0.7 constant_dynamic-update-slice_fusion.4
  392.8 1.7 collective-permute-done.10
  394.5 0.7 constant_dynamic-update-slice_fusion.3
  395.8 0.7 constant_dynamic-update-slice_fusion.1
  396.5 0.7 constant_dynamic-update-slice_fusion
  397.8 1.7 reshape_reshape.7
  399.5 1.1 gather_fusion.1
  401.5 43.0 %all-reduce = f32[7168]{0:T(1024)S(1)} all-reduce(f32[7168]{0:T(1024)S(1)} %get-tuple-element.6), channel_id=4, replica_groups=mesh['seq'=2,'ep'=16] {'seq','ep'}, use_global_device_ids=true, to_apply=%region_12.13.clone | all-reduce | flops 7168 | bytes 57344
  445.2 0.8 fusion.33
  446.0 1.7 reshape.128
  447.7 1.1 gather_fusion
  448.8 1.4 fusion.14
  (65 shorter events, 8.0 us)
Async XLA Ops:
  16.9 7.5 %copy-start.9 = (s32[8,8]{1,0:T(8,128)S(1)}, s32[8,8]{1,0:T(8,128)}, u32[]{:S(2)}) copy-start(s32[8,8]{1,0:T(8,128)} %param.12) | copy-start | bytes 772
  16.9 7.6 %copy-start.2 = (bf16[8,7168]{1,0:T(8,128)(2,1)S(1)}, bf16[8,7168]{1,0:T(8,128)(2,1)}, u32[]{:S(2)}) copy-start(bf16[8,7168]{1,0:T(8,128)(2,1)} %param.10) | copy-start | bytes 344068
  16.9 91.0 %all-to-all-start = ((bf16[32,5,7168]{2,1,0:T(8,128)(2,1)}), bf16[32,5,7168]{2,1,0:T(8,128)(2,1)}, u32[]{:S(2)}, u32[]{:S(2)}) async-start(bf16[32,5,7168]{2,1,0:T(8,128)(2,1)} %bitcast.66), calls=%async_computation | async-start | bytes 7340032 | tf_op jit(solution)/shard_map/all_to_all | solution.py:57
  110.4 87.2 %all-to-all-start.2 = ((bf16[32,5,7168]{2,1,0:T(8,128)(2,1)}), bf16[32,5,7168]{2,1,0:T(8,128)(2,1)}, u32[]{:S(2)}, u32[]{:S(2)}) async-start(bf16[32,5,7168]{2,1,0:T(8,128)(2,1)} %bitcast.67), calls=%async_computation.3 | async-start | bytes 7340032 | tf_op jit(solution)/shard_map/all_to_all | solution.py:58
  113.9 135.9 %reduce-scatter.5.cloned.1.call-start = ((), (), s32[]{:S(2)}) async-start(), calls=%async_computation.6 | async-start | bytes 3440640 | tf_op jit(solution)/shard_map/reduce_scatter | solution.py:72
  202.1 12.4 %slice-start = ((s8[7340032]{0:T(1024)(128)(4,1)}), s8[4194304]{0:T(1024)(128)(4,1)S(1)}, s32[]{:S(2)}) async-start(s8[7340032]{0:T(1024)(128)(4,1)} %bitcast.64), calls=%async_computation.7 | async-start | bytes 8388608
  208.7 5.8 %slice-start.1 = ((s8[7340032]{0:T(1024)(128)(4,1)}), s8[3145728]{0:T(1024)(128)(4,1)S(1)}, s32[]{:S(2)}) async-start(s8[7340032]{0:T(1024)(128)(4,1)} %bitcast.64), calls=%async_computation.8 | async-start | bytes 6291456
  218.5 67.6 %reduce-scatter.3.cloned.1.call-start = ((), (), s32[]{:S(2)}) async-start(), calls=%async_computation.5 | async-start | bytes 3440640 | tf_op jit(solution)/shard_map/reduce_scatter | solution.py:66
  253.3 6.9 %collective-permute-start = (bf16[1,1,5,7168]{3,2,0,1:T(8,128)(2,1)S(1)}, bf16[1,1,5,7168]{3,2,0,1:T(8,128)(2,1)S(1)}, u32[]{:S(2)}, u32[]{:S(2)}) collective-permute-start(bf16[1,1,5,7168]{3,2,0,1:T(8,128)(2,1)S(1)} %constant_dynamic-slice_fusion.14), channel_id=1, source_target_pairs={{0,1},{1,2},{2,3},{3,4},{4,5},{5,6},{6,7},{7,8},{8,9},{9,10},{10,1... | collective-permute-start | bytes 215048 | tf_op jit(solution)/shard_map/ppermute | solution.py:30
  262.6 37.5 %collective-permute-start.1 = (bf16[1,1,5,7168]{3,2,0,1:T(8,128)(2,1)}, bf16[1,1,5,7168]{3,2,0,1:T(8,128)(2,1)S(1)}, u32[]{:S(2)}, u32[]{:S(2)}) collective-permute-start(bf16[1,1,5,7168]{3,2,0,1:T(8,128)(2,1)} %get-tuple-element.23), channel_id=1, source_target_pairs={{0,2},{1,3},{2,4},{3,5},{4,6},{5,7},{6,8},{7,9},{8,10},{9,11},{10,... | collective-permute-start | bytes 215048 | tf_op jit(solution)/shard_map/ppermute | solution.py:30
  288.7 11.4 %copy-start.8 = (bf16[1,1,5,7168]{3,2,0,1:T(8,128)(2,1)S(1)}, bf16[1,1,5,7168]{3,2,0,1:T(8,128)(2,1)}, u32[]{:S(2)}) copy-start(bf16[1,1,5,7168]{3,2,0,1:T(8,128)(2,1)} %get-tuple-element.22) | copy-start | bytes 215044
  288.7 49.6 %copy-start.7 = (bf16[1,1,5,7168]{3,2,0,1:T(8,128)(2,1)S(1)}, bf16[1,1,5,7168]{3,2,0,1:T(8,128)(2,1)}, u32[]{:S(2)}) copy-start(bf16[1,1,5,7168]{3,2,0,1:T(8,128)(2,1)} %get-tuple-element.21) | copy-start | bytes 215044
  288.7 56.3 %copy-start.6 = (bf16[1,1,5,7168]{3,2,0,1:T(8,128)(2,1)S(1)}, bf16[1,1,5,7168]{3,2,0,1:T(8,128)(2,1)}, u32[]{:S(2)}) copy-start(bf16[1,1,5,7168]{3,2,0,1:T(8,128)(2,1)} %get-tuple-element.20) | copy-start | bytes 215044
  288.7 63.8 %copy-start.5 = (bf16[1,1,5,7168]{3,2,0,1:T(8,128)(2,1)S(1)}, bf16[1,1,5,7168]{3,2,0,1:T(8,128)(2,1)}, u32[]{:S(2)}) copy-start(bf16[1,1,5,7168]{3,2,0,1:T(8,128)(2,1)} %get-tuple-element.19) | copy-start | bytes 215044
  288.7 71.9 %copy-start.4 = (bf16[1,1,5,7168]{3,2,0,1:T(8,128)(2,1)S(1)}, bf16[1,1,5,7168]{3,2,0,1:T(8,128)(2,1)}, u32[]{:S(2)}) copy-start(bf16[1,1,5,7168]{3,2,0,1:T(8,128)(2,1)} %get-tuple-element.18) | copy-start | bytes 215044
  288.7 77.0 %copy-start.3 = (bf16[1,1,5,7168]{3,2,0,1:T(8,128)(2,1)S(1)}, bf16[1,1,5,7168]{3,2,0,1:T(8,128)(2,1)}, u32[]{:S(2)}) copy-start(bf16[1,1,5,7168]{3,2,0,1:T(8,128)(2,1)} %get-tuple-element.17) | copy-start | bytes 215044
  288.8 157.2 %all-to-all-start.1 = ((bf16[16,5,7168]{2,1,0:T(8,128)(2,1)}), bf16[16,5,7168]{2,1,0:T(8,128)(2,1)}, u32[]{:S(2)}, u32[]{:S(2)}) async-start(bf16[16,5,7168]{2,1,0:T(8,128)(2,1)} %reshape.127), calls=%async_computation.2 | async-start | bytes 3670016 | tf_op jit(solution)/shard_map/all_to_all | solution.py:80
  294.6 102.6 %collective-permute-start.14 = (bf16[1,1,5,7168]{3,2,0,1:T(8,128)(2,1)S(1)}, bf16[1,1,5,7168]{3,2,0,1:T(8,128)(2,1)S(1)}, u32[]{:S(2)}, u32[]{:S(2)}) collective-permute-start(bf16[1,1,5,7168]{3,2,0,1:T(8,128)(2,1)S(1)} %get-tuple-element.10), channel_id=1, source_target_pairs={{0,15},{1,0},{2,1},{3,2},{4,3},{5,4},{6,5},{7,6},{8,7},{9,8},{10,9... | collective-permute-start | bytes 215048 | tf_op jit(solution)/shard_map/ppermute | solution.py:30
  298.9 97.6 %collective-permute-start.13 = (bf16[1,1,5,7168]{3,2,0,1:T(8,128)(2,1)S(1)}, bf16[1,1,5,7168]{3,2,0,1:T(8,128)(2,1)S(1)}, u32[]{:S(2)}, u32[]{:S(2)}) collective-permute-start(bf16[1,1,5,7168]{3,2,0,1:T(8,128)(2,1)S(1)} %get-tuple-element.11), channel_id=1, source_target_pairs={{0,14},{1,15},{2,0},{3,1},{4,2},{5,3},{6,4},{7,5},{8,6},{9,7},{10,... | collective-permute-start | bytes 215048 | tf_op jit(solution)/shard_map/ppermute | solution.py:30
  299.4 96.4 %collective-permute-start.12 = (bf16[1,1,5,7168]{3,2,0,1:T(8,128)(2,1)S(1)}, bf16[1,1,5,7168]{3,2,0,1:T(8,128)(2,1)S(1)}, u32[]{:S(2)}, u32[]{:S(2)}) collective-permute-start(bf16[1,1,5,7168]{3,2,0,1:T(8,128)(2,1)S(1)} %get-tuple-element.12), channel_id=1, source_target_pairs={{0,13},{1,14},{2,15},{3,0},{4,1},{5,2},{6,3},{7,4},{8,5},{9,6},{10... | collective-permute-start | bytes 215048 | tf_op jit(solution)/shard_map/ppermute | solution.py:30
  299.5 95.6 %collective-permute-start.11 = (bf16[1,1,5,7168]{3,2,0,1:T(8,128)(2,1)S(1)}, bf16[1,1,5,7168]{3,2,0,1:T(8,128)(2,1)S(1)}, u32[]{:S(2)}, u32[]{:S(2)}) collective-permute-start(bf16[1,1,5,7168]{3,2,0,1:T(8,128)(2,1)S(1)} %get-tuple-element.13), channel_id=1, source_target_pairs={{0,12},{1,13},{2,14},{3,15},{4,0},{5,1},{6,2},{7,3},{8,4},{9,5},{1... | collective-permute-start | bytes 215048 | tf_op jit(solution)/shard_map/ppermute | solution.py:30
  300.1 38.2 %collective-permute-start.2 = (bf16[1,1,5,7168]{3,2,0,1:T(8,128)(2,1)S(1)}, bf16[1,1,5,7168]{3,2,0,1:T(8,128)(2,1)S(1)}, u32[]{:S(2)}, u32[]{:S(2)}) collective-permute-start(bf16[1,1,5,7168]{3,2,0,1:T(8,128)(2,1)S(1)} %copy-done.8), channel_id=1, source_target_pairs={{0,3},{1,4},{2,5},{3,6},{4,7},{5,8},{6,9},{7,10},{8,11},{9,12},{10... | collective-permute-start | bytes 215048 | tf_op jit(solution)/shard_map/ppermute | solution.py:30
  338.3 6.7 %collective-permute-start.3 = (bf16[1,1,5,7168]{3,2,0,1:T(8,128)(2,1)S(1)}, bf16[1,1,5,7168]{3,2,0,1:T(8,128)(2,1)S(1)}, u32[]{:S(2)}, u32[]{:S(2)}) collective-permute-start(bf16[1,1,5,7168]{3,2,0,1:T(8,128)(2,1)S(1)} %copy-done.7), channel_id=1, source_target_pairs={{0,4},{1,5},{2,6},{3,7},{4,8},{5,9},{6,10},{7,11},{8,12},{9,13},{1... | collective-permute-start | bytes 215048 | tf_op jit(solution)/shard_map/ppermute | solution.py:30
  345.0 7.5 %collective-permute-start.4 = (bf16[1,1,5,7168]{3,2,0,1:T(8,128)(2,1)S(1)}, bf16[1,1,5,7168]{3,2,0,1:T(8,128)(2,1)S(1)}, u32[]{:S(2)}, u32[]{:S(2)}) collective-permute-start(bf16[1,1,5,7168]{3,2,0,1:T(8,128)(2,1)S(1)} %copy-done.6), channel_id=1, source_target_pairs={{0,5},{1,6},{2,7},{3,8},{4,9},{5,10},{6,11},{7,12},{8,13},{9,14},{... | collective-permute-start | bytes 215048 | tf_op jit(solution)/shard_map/ppermute | solution.py:30
  352.5 8.2 %collective-permute-start.5 = (bf16[1,1,5,7168]{3,2,0,1:T(8,128)(2,1)S(1)}, bf16[1,1,5,7168]{3,2,0,1:T(8,128)(2,1)S(1)}, u32[]{:S(2)}, u32[]{:S(2)}) collective-permute-start(bf16[1,1,5,7168]{3,2,0,1:T(8,128)(2,1)S(1)} %copy-done.5), channel_id=1, source_target_pairs={{0,6},{1,7},{2,8},{3,9},{4,10},{5,11},{6,12},{7,13},{8,14},{9,15},... | collective-permute-start | bytes 215048 | tf_op jit(solution)/shard_map/ppermute | solution.py:30
  360.7 5.1 %collective-permute-start.6 = (bf16[1,1,5,7168]{3,2,0,1:T(8,128)(2,1)S(1)}, bf16[1,1,5,7168]{3,2,0,1:T(8,128)(2,1)S(1)}, u32[]{:S(2)}, u32[]{:S(2)}) collective-permute-start(bf16[1,1,5,7168]{3,2,0,1:T(8,128)(2,1)S(1)} %copy-done.4), channel_id=1, source_target_pairs={{0,7},{1,8},{2,9},{3,10},{4,11},{5,12},{6,13},{7,14},{8,15},{9,0},... | collective-permute-start | bytes 215048 | tf_op jit(solution)/shard_map/ppermute | solution.py:30
  365.8 11.4 %collective-permute-start.7 = (bf16[1,1,5,7168]{3,2,0,1:T(8,128)(2,1)S(1)}, bf16[1,1,5,7168]{3,2,0,1:T(8,128)(2,1)S(1)}, u32[]{:S(2)}, u32[]{:S(2)}) collective-permute-start(bf16[1,1,5,7168]{3,2,0,1:T(8,128)(2,1)S(1)} %copy-done.3), channel_id=1, source_target_pairs={{0,8},{1,9},{2,10},{3,11},{4,12},{5,13},{6,14},{7,15},{8,0},{9,1},... | collective-permute-start | bytes 215048 | tf_op jit(solution)/shard_map/ppermute | solution.py:30
  377.1 5.1 %collective-permute-start.8 = (bf16[1,1,5,7168]{3,2,0,1:T(8,128)(2,1)S(1)}, bf16[1,1,5,7168]{3,2,0,1:T(8,128)(2,1)S(1)}, u32[]{:S(2)}, u32[]{:S(2)}) collective-permute-start(bf16[1,1,5,7168]{3,2,0,1:T(8,128)(2,1)S(1)} %get-tuple-element.16), channel_id=1, source_target_pairs={{0,9},{1,10},{2,11},{3,12},{4,13},{5,14},{6,15},{7,0},{8,1},{9,2},... | collective-permute-start | bytes 215048 | tf_op jit(solution)/shard_map/ppermute | solution.py:30
  382.3 6.1 %collective-permute-start.9 = (bf16[1,1,5,7168]{3,2,0,1:T(8,128)(2,1)S(1)}, bf16[1,1,5,7168]{3,2,0,1:T(8,128)(2,1)S(1)}, u32[]{:S(2)}, u32[]{:S(2)}) collective-permute-start(bf16[1,1,5,7168]{3,2,0,1:T(8,128)(2,1)S(1)} %get-tuple-element.15), channel_id=1, source_target_pairs={{0,10},{1,11},{2,12},{3,13},{4,14},{5,15},{6,0},{7,1},{8,2},{9,3},... | collective-permute-start | bytes 215048 | tf_op jit(solution)/shard_map/ppermute | solution.py:30
  388.4 6.1 %collective-permute-start.10 = (bf16[1,1,5,7168]{3,2,0,1:T(8,128)(2,1)S(1)}, bf16[1,1,5,7168]{3,2,0,1:T(8,128)(2,1)S(1)}, u32[]{:S(2)}, u32[]{:S(2)}) collective-permute-start(bf16[1,1,5,7168]{3,2,0,1:T(8,128)(2,1)S(1)} %get-tuple-element.14), channel_id=1, source_target_pairs={{0,11},{1,12},{2,13},{3,14},{4,15},{5,0},{6,1},{7,2},{8,3},{9,4},{... | collective-permute-start | bytes 215048 | tf_op jit(solution)/shard_map/ppermute | solution.py:30
  399.5 1.8 copy-start
  399.5 1.8 copy-start.1
Sparse Core Ops, SparseCore 0:
  218.7 31.0 reduce-scatter.4
  252.0 34.0 reduce-scatter.2
